TPU v7x, 32 devices: a whole 2x2x4 slice. The times are simulated.
32 devices in a mesh: phase: 2 (over core), tok: 4 (over z), mp: 4 (over y, x).
Axes of the slice: x: 2, y: 2, z: 4, core: 2. Of those that a mesh axis runs over, the one named last changes fastest.
Arguments:
- hidden: bfloat16 [2, 512, 6656], P('phase', 'tok', 'mp'), may hold values from -30 to 30
- w_qkv: bfloat16 [2, 6656, 3, 4096], P('phase', 'mp', None, 'tok'), may hold values from -1 to 1
- segment_ids: int32 [2, 512], P('phase'), may hold values from 0 to 3, never falling along the last dimension, each value on 1 to 256 neighbouring positions
- exit_flags: int32 [2, 4], P('phase'), may hold values from 0 to 1, as said below
Outputs:
- attended: bfloat16 [2, 512, 4096], P('phase', 'mp', 'tok')
- handed: bfloat16 [2, 512, 4096], P('phase', 'mp', 'tok')
Inputs may be any that keep to these rules, and one draw needn't show every extreme that they name: `exit_flags`: in each micro-batch exactly 2 of the 4 blocks have flag 0.
All inputs are finite; a program needn't handle non-finite values.
Results may differ from a plain program's by a relative error of at most 0.0068.
Values may be sent and summed in bfloat16 or wider, within the bound.
A program may use at most 64 MiB of HBM per device.

v0:
```python
import math
import jax
import jax.numpy as jnp
from jax import lax
from jax.sharding import PartitionSpec as P

HEAD = 128
BLOCK = 128


def shifted(block, axis, distance):
    devices = range(lax.axis_size(axis))
    route = [((i - distance) % len(devices), i) for i in devices]
    return lax.ppermute(block, axis, route)


def attend(query, keys, values, query_pos, segment, key_pos):
    heads_here = query.shape[1] // HEAD
    total = keys.shape[0]
    key_heads = keys.reshape(total, heads_here, HEAD)
    value_heads = values.reshape(total, heads_here, HEAD)
    key_segment = jnp.take(segment, key_pos)
    scale = 1.0 / math.sqrt(HEAD)
    block_rows = query.shape[0]
    scores = (
        jnp.einsum(
            "rhd,shd->hrs",
            query.reshape(block_rows, heads_here, HEAD),
            key_heads,
            preferred_element_type=jnp.float32,
        )
        * scale
    )
    own_segment = jnp.take(segment, query_pos)
    allowed = (key_pos[None, :] <= query_pos[:, None]) & (
        key_segment[None, :] == own_segment[:, None]
    )
    scores = jnp.where(allowed[None], scores, -1e30)
    peak = jnp.max(scores, axis=-1, keepdims=True)
    expo = jnp.exp(scores - peak)
    probs = (expo / jnp.sum(expo, axis=-1, keepdims=True)).astype(jnp.bfloat16)
    mixed = jnp.einsum("hrs,shd->rhd", probs, value_heads, preferred_element_type=jnp.float32)
    return mixed.reshape(block_rows, heads_here * HEAD).astype(jnp.bfloat16)


def local(hidden, w_qkv, segment_ids, exit_flags):
    rows_here = hidden[0]
    weights = w_qkv[0]
    width_here = rows_here.shape[1]
    head_cols = weights.shape[2]
    flat_weights = weights.reshape(width_here, 3 * head_cols)
    segment = segment_ids[0]
    flags = exit_flags[0]
    groups = lax.axis_size("mp")
    member = lax.axis_index("mp")
    partial_value = jnp.dot(
        lax.all_gather(rows_here, "tok", axis=0, tiled=True),
        flat_weights,
        preferred_element_type=jnp.float32,
    )
    total = partial_value.shape[0]
    quarter = total // groups
    query_part = partial_value[:, :head_cols]
    key_value_part = partial_value[:, head_cols:]
    my_pos = member * quarter + jnp.arange(quarter, dtype=jnp.int32)
    my_blocks = my_pos // BLOCK
    alive = jnp.take(flags, my_blocks) == 0
    query = lax.psum_scatter(query_part, "mp", scatter_dimension=0, tiled=True).astype(jnp.bfloat16)
    mine = lax.psum_scatter(key_value_part, "mp", scatter_dimension=0, tiled=True).astype(
        jnp.bfloat16
    )
    key_value = lax.all_gather(mine, "mp", axis=0, tiled=True)
    all_pos = jnp.arange(total, dtype=jnp.int32)
    mixed = attend(
        query, key_value[:, :head_cols], key_value[:, head_cols:], my_pos, segment, all_pos
    )
    zeros = jnp.zeros((quarter, head_cols), jnp.bfloat16)
    result = jnp.where(alive[:, None], mixed, zeros)
    handed = shifted(result, "phase", 1)
    return (result[None], handed[None])


def solution(mesh):
    in_specs = (
        P("phase", "tok", "mp"),
        P("phase", "mp", None, "tok"),
        P("phase", None),
        P("phase", None),
    )
    out_specs = (P("phase", "mp", "tok"), P("phase", "mp", "tok"))
    return jax.shard_map(local, mesh=mesh, in_specs=in_specs, out_specs=out_specs, check_vma=False)
```

profile of v0, /device:TPU:0, one launch (start us, length us, event | category | flops | bytes accessed | tf_op | source)
XLA Modules:
  0.0 207.5 jit_solution(11496909522336261351)
XLA Ops:
  7.2 0.0 all-gather.6.cloned.1.call-start
  7.2 0.7 all-gather.6.cloned.1.call-update
  7.9 0.0 reduce-scatter.3.cloned.1.call-start
  8.0 13.5 %copy.11 = bf16[1,1664,3,1024]{1,3,2,0:T(8,128)(2,1)} copy(bf16[1,1664,3,1024]{3,1,2,0:T(8,128)(2,1)} %param.5) | data formatting | bytes 20447232 | tf_op args[1]
  21.5 30.0 %all-gather.6.cloned.1.call-done = bf16[1,512,1664]{2,1,0:T(8,128)(2,1)} async-done(((bf16[1,128,1664]{2,1,0:T(8,128)(2,1)}), bf16[1,512,1664]{2,1,0:T(8,128)(2,1)}) %all-gather.6.cloned.1.call-update) | async-done | bytes 1703952 | tf_op jit(solution)/shard_map/all_gather | solution.py:57
  51.5 9.1 %fusion.2 = f32[512,3072]{1,0:T(8,128)S(1)} fusion(bf16[1664,3072]{0,1:T(8,128)(2,1)} %bitcast.57, bf16[1,512,1664]{2,1,0:T(8,128)(2,1)} %all-gather.6.cloned.1.call-done), kind=kOutput, calls=%fused_computation.7 | convolution fusion | flops 5234491392 | bytes 18219008 | tf_op jit(solution)/shard_map/dot_general | solution.py:56
  60.6 2.7 %copy-done.1 = f32[512,3072]{1,0:T(8,128)} copy-done((f32[512,3072]{1,0:T(8,128)}, f32[512,3072]{1,0:T(8,128)S(1)}, u32[]{:S(2)}) %copy-start.1) | copy-done | bytes 6291480
  63.3 2.5 %slice.30 = f32[512,2048]{1,0:T(8,128)} slice(f32[512,3072]{1,0:T(8,128)S(1)} %fusion.2), slice={[0:512], [1024:3072]} | slice | bytes 8388608 | tf_op jit(solution)/shard_map/slice | solution.py:64
  65.8 0.0 reduce-scatter.3.cloned.1.call-update
  65.8 0.0 all-gather.4.cloned.1.call-start
  65.9 51.5 %reduce-scatter.3.cloned.1.call-done = f32[128,2048]{1,0:T(8,128)} async-done(((f32[512,2048]{1,0:T(8,128)}), f32[128,2048]{1,0:T(8,128)}) %reduce-scatter.3.cloned.1.call-update) | async-done | bytes 1048592 | tf_op jit(solution)/shard_map/reduce_scatter | solution.py:69
  117.4 2.1 %convert_element_type.29 = bf16[128,2048]{1,0:T(8,128)(2,1)} convert(f32[128,2048]{1,0:T(8,128)} %reduce-scatter.3.cloned.1.call-done) | non-fusion elementwise | flops 262144 | bytes 1572864 | tf_op jit(solution)/shard_map/convert_element_type | solution.py:69
  119.5 0.0 reduce-scatter.5.cloned.1.call-start
  119.6 3.2 %slice.32 = f32[512,1024]{1,0:T(8,128)} slice(f32[512,3072]{1,0:T(8,128)} %copy-done.1), slice={[0:512], [0:1024]} | slice | bytes 4194304 | tf_op jit(solution)/shard_map/slice | solution.py:63
  122.8 3.5 %gather_fusion = s32[512]{0:T(512)S(1)} fusion(s32[512]{0:T(512)S(1)} %bitcast.55, s32[1024]{0:T(1024)S(1)} %pad_clamp_fusion.1), kind=kCustom, calls=%fused_computation | custom fusion | bytes 6144 | tf_op jit(solution)/shard_map/jit(_take)/gather | solution.py:22
  126.4 1.3 gather_fusion.1
  127.7 0.7 fusion.31
  128.3 2.6 %fusion.28 = pred[128]{0:T(512)(128)(4,1)S(1)} fusion(s32[]{:T(128)} %bitcast, s32[]{:T(128)} %bitcast.1, s32[]{:T(128)} %bitcast.3, s32[]{:T(128)} %bitcast.2, s32[]{:T(128)S(6)} %mul.9), kind=kLoop, calls=%fused_computation.48 | loop fusion | flops 6272 | bytes 148 | tf_op jit(solution)/shard_map/eq | solution.py:67
  130.9 0.1 fusion.12
  131.0 23.8 %all-gather.4.cloned.1.call-done = bf16[512,2048]{1,0:T(8,128)(2,1)} async-done(((bf16[128,2048]{1,0:T(8,128)(2,1)}), bf16[512,2048]{1,0:T(8,128)(2,1)}) %all-gather.4.cloned.1.call-update) | async-done | bytes 2097168 | tf_op jit(solution)/shard_map/all_gather | solution.py:72
  154.9 1.7 slice_bitcast_fusion
  156.6 0.5 copy.17
  157.2 35.7 %reduce-scatter.5.cloned.1.call-done = f32[128,1024]{1,0:T(8,128)} async-done(((f32[512,1024]{1,0:T(8,128)}), f32[128,1024]{1,0:T(8,128)}) %reduce-scatter.5.cloned.1.call-update) | async-done | bytes 524304 | tf_op jit(solution)/shard_map/reduce_scatter | solution.py:68
  192.9 3.3 %fusion.32 = (f32[8,128]{1,0:T(8,128)S(1)}, f32[8,128,512]{2,1,0:T(8,128)}) fusion(pred[128,512]{1,0:T(8,128)(4,1)S(1)} %fusion.12, bf16[64,8,8,128]{3,2,1,0:T(8,128)(2,1)S(1)} %get-tuple-element.2, f32[128,1024]{1,0:T(8,128)} %reduce-scatter.5.cloned.1.call-done), kind=kOutput, calls=%fused_computation.53 | convolution fusion | flops 136446464 | bytes 3739648 | tf_op jit(solution)/shard_map/sub | solution.py:40
  196.2 2.2 %convolution_convert_fusion = bf16[8,128,128]{2,1,0:T(8,128)(2,1)S(1)} fusion(bf16[512,8,128]{0,2,1:T(8,128)(2,1)S(1)} %bitcast.58, f32[8,128,512]{2,1,0:T(8,128)} %get-tuple-element.9, f32[8,128]{1,0:T(8,128)S(1)} %get-tuple-element.8), kind=kOutput, calls=%fused_computation.9 | convolution fusion | flops 135397376 | bytes 3411968 | tf_op jit(solution)/shard_map/hrs,shd->rhd/dot_general | solution.py:42
  198.4 0.1 copy.16
  198.6 0.1 broadcast_select_fusion
  198.6 0.1 collective-permute-start
  198.7 0.1 copy.15
  198.9 0.8 broadcast_select_fusion.1
  199.7 0.6 collective-permute-done
  200.2 0.7 copy.45
  (13 shorter events, 0.1 us)
Async XLA Ops:
  7.2 115.7 %copy-start = (s32[1,512]{1,0:T(1,128)S(1)}, s32[1,512]{1,0:T(1,128)}, u32[]{:S(2)}) copy-start(s32[1,512]{1,0:T(1,128)} %param.6) | copy-start | bytes 6148
  7.2 44.3 %all-gather.6.cloned.1.call-start = ((), (), s32[]{:S(2)}) async-start(), calls=%async_computation.5 | async-start | bytes 2129920 | tf_op jit(solution)/shard_map/all_gather | solution.py:57
  7.9 109.5 %reduce-scatter.3.cloned.1.call-start = ((), (), s32[]{:S(2)}) async-start(), calls=%async_computation.2 | async-start | bytes 5242880 | tf_op jit(solution)/shard_map/reduce_scatter | solution.py:69
  60.6 2.7 %copy-start.1 = (f32[512,3072]{1,0:T(8,128)}, f32[512,3072]{1,0:T(8,128)S(1)}, u32[]{:S(2)}) copy-start(f32[512,3072]{1,0:T(8,128)S(1)} %fusion.2) | copy-start | bytes 18874372
  65.8 89.1 %all-gather.4.cloned.1.call-start = ((), (), s32[]{:S(2)}) async-start(), calls=%async_computation.3 | async-start | bytes 2621440 | tf_op jit(solution)/shard_map/all_gather | solution.py:72
  119.5 73.4 %reduce-scatter.5.cloned.1.call-start = ((), (), s32[]{:S(2)}) async-start(), calls=%async_computation.4 | async-start | bytes 2621440 | tf_op jit(solution)/shard_map/reduce_scatter | solution.py:68
  122.8 4.9 %copy-start.2 = (s32[1,4]{1,0:T(1,128)S(1)}, s32[1,4]{1,0:T(1,128)}, u32[]{:S(2)}) copy-start(s32[1,4]{1,0:T(1,128)} %param.7) | copy-start | bytes 52
  198.6 1.6 collective-permute-start
Sparse Core Ops, SparseCore 0:
  9.6 41.8 all-gather.5
  65.9 51.4 reduce-scatter.2
  119.6 35.1 all-gather.3
  157.7 35.1 reduce-scatter.4
where the time goes:
time: 208 us; the launch traced here: 207 us
  waiting for transfers between devices  142 us (68%)
  local copies, waits for them, and re-layouts  30.7 us (15%)
  matrix products  14.6 us (7%)
  between operations  13.9 us (7%)
  other arithmetic  5.68 us (3%)
    reduce_scatter x1, waiting for transfers between devices, local(): lax.psum_scatter(key_value_part, 'mp', scatter_dimension=0, tiled=True)  51.5 us
    reduce_scatter x1, waiting for transfers between devices, local(): lax.psum_scatter(query_part, 'mp', scatter_dimension=0, tiled=True)  35.7 us
    all_gather x1, waiting for transfers between devices, local(): lax.all_gather(rows_here, 'tok', axis=0, tiled=True)  30 us
    all_gather x1, waiting for transfers between devices, local(): key_value = lax.all_gather(mine, 'mp', axis=0, tiled=True)  23.8 us
    unnamed x9, local copies, waits for them, and re-layouts  18.7 us
    dot_general x1, matrix products, local(): jnp.dot(lax.all_gather(rows_here, 'tok', axis=0, tiled=True), flat_weight...  9.08 us
  transfers between devices with their start and end apart: 5, of which 5 were waited for; matrix products, arithmetic and copies ran while one was open for 14% of the time, Pallas kernels for 0%

commit v1 on v0

--- a/solution.py
+++ b/solution.py
@@ -69,7 +69,12 @@
     mine = lax.psum_scatter(key_value_part, "mp", scatter_dimension=0, tiled=True).astype(
         jnp.bfloat16
     )
-    key_value = lax.all_gather(mine, "mp", axis=0, tiled=True)
+    ring = [mine]
+    for hop in range(3):
+        ring.append(lax.ppermute(ring[-1], "mp", [(dev, (dev + 1) % 4) for dev in range(4)]))
+    key_value = jnp.roll(
+        jnp.concatenate(ring[::-1], axis=0), (lax.axis_index("mp") + 1) * ring[0].shape[0], axis=0
+    )
     all_pos = jnp.arange(total, dtype=jnp.int32)
     mixed = attend(
         query, key_value[:, :head_cols], key_value[:, head_cols:], my_pos, segment, all_pos

time: 208 us -> 191 us (0.918)
  waiting for transfers between devices: 142 us -> 123 us
  starting transfers between devices: 0.23 us -> 4.3 us
    ppermute x0 -> x3, waiting for transfers between devices: none -> 43.5 us  [local(): lax.ppermute(ring[-1], 'mp', [(dev, (dev + 1) % 4) for dev in range(4)])]
    reduce_scatter x1, waiting for transfers between devices: 35.7 us -> 0.02 us  [local(): lax.psum_scatter(query_part, 'mp', scatter_dimension=0, tiled=True)]
    all_gather x1 -> x0, waiting for transfers between devices: 23.8 us -> none  [local(): key_value = lax.all_gather(mine, 'mp', axis=0, tiled=True)]
    ppermute x0 -> x3, starting transfers between devices: none -> 4.12 us  [local(): lax.ppermute(ring[-1], 'mp', [(dev, (dev + 1) % 4) for dev in range(4)])]
    reduce_scatter x1, waiting for transfers between devices: 51.5 us -> 48.3 us  [local(): lax.psum_scatter(key_value_part, 'mp', scatter_dimension=0, tiled=True)]
    unnamed x9 -> x17, local copies, waits for them, and re-layouts: 18.7 us -> 17.3 us
  transfers between devices with their start and end apart: 5 -> 7, of which waited for: 5 -> 6; matrix products, arithmetic and copies ran while one was open for 14% -> 15% of each run, Pallas kernels for 0% -> 0%
where the time goes in v1:
time: 191 us; the launch traced here: 190 us
  waiting for transfers between devices  123 us (64%)
  local copies, waits for them, and re-layouts  29.2 us (15%)
  matrix products  14.6 us (8%)
  between operations  14 us (7%)
  other arithmetic  5.09 us (3%)
  starting transfers between devices  4.3 us (2%)
    reduce_scatter x1, waiting for transfers between devices, local(): lax.psum_scatter(key_value_part, 'mp', scatter_dimension=0, tiled=True)  48.3 us
    ppermute x3, waiting for transfers between devices, local(): lax.ppermute(ring[-1], 'mp', [(dev, (dev + 1) % 4) for dev in range(4)])  43.5 us
    all_gather x1, waiting for transfers between devices, local(): lax.all_gather(rows_here, 'tok', axis=0, tiled=True)  30.1 us
    unnamed x17, local copies, waits for them, and re-layouts  17.3 us
    dot_general x1, matrix products, local(): jnp.dot(lax.all_gather(rows_here, 'tok', axis=0, tiled=True), flat_weight...  9.08 us
    ppermute x3, starting transfers between devices, local(): lax.ppermute(ring[-1], 'mp', [(dev, (dev + 1) % 4) for dev in range(4)])  4.12 us
  transfers between devices with their start and end apart: 7, of which 6 were waited for; matrix products, arithmetic and copies ran while one was open for 15% of the time, Pallas kernels for 0%

profile of v1, /device:TPU:0, one launch (start us, length us, event | category | flops | bytes accessed | tf_op | source)
XLA Modules:
  0.0 190.4 jit_solution(2997901641505146020)
XLA Ops:
  7.2 0.7 all-gather.3.cloned.1.call-update
  8.0 13.5 %copy.11 = bf16[1,1664,3,1024]{1,3,2,0:T(8,128)(2,1)} copy(bf16[1,1664,3,1024]{3,1,2,0:T(8,128)(2,1)} %param.5) | data formatting | bytes 20447232 | tf_op args[1]
  21.4 30.1 %all-gather.3.cloned.1.call-done = bf16[1,512,1664]{2,1,0:T(8,128)(2,1)} async-done(((bf16[1,128,1664]{2,1,0:T(8,128)(2,1)}), bf16[1,512,1664]{2,1,0:T(8,128)(2,1)}) %all-gather.3.cloned.1.call-update) | async-done | bytes 1703952 | tf_op jit(solution)/shard_map/all_gather | solution.py:57
  51.5 9.1 %fusion.2 = f32[512,3072]{1,0:T(8,128)S(1)} fusion(bf16[1664,3072]{0,1:T(8,128)(2,1)} %bitcast.57, bf16[1,512,1664]{2,1,0:T(8,128)(2,1)} %all-gather.3.cloned.1.call-done), kind=kOutput, calls=%fused_computation.7 | convolution fusion | flops 5234491392 | bytes 18219008 | tf_op jit(solution)/shard_map/dot_general | solution.py:56
  60.6 2.7 %copy-done.2 = f32[512,3072]{1,0:T(8,128)} copy-done((f32[512,3072]{1,0:T(8,128)}, f32[512,3072]{1,0:T(8,128)S(1)}, u32[]{:S(2)}) %copy-start.2) | copy-done | bytes 6291480
  63.2 2.5 %slice.30 = f32[512,2048]{1,0:T(8,128)} slice(f32[512,3072]{1,0:T(8,128)S(1)} %fusion.2), slice={[0:512], [1024:3072]} | slice | bytes 8388608 | tf_op jit(solution)/shard_map/slice | solution.py:64
  65.8 3.2 %slice.31 = f32[512,1024]{1,0:T(8,128)} slice(f32[512,3072]{1,0:T(8,128)} %copy-done.2), slice={[0:512], [0:1024]} | slice | bytes 4194304 | tf_op jit(solution)/shard_map/slice | solution.py:63
  69.0 48.3 %reduce-scatter.3.cloned.1.call-done = f32[128,2048]{1,0:T(8,128)} async-done(((f32[512,2048]{1,0:T(8,128)}), f32[128,2048]{1,0:T(8,128)}) %reduce-scatter.3.cloned.1.call-update) | async-done | bytes 1048592 | tf_op jit(solution)/shard_map/reduce_scatter | solution.py:69
  117.4 1.4 convert_element_type.29
  118.8 1.5 collective-permute-start
  120.3 17.7 %collective-permute-done = bf16[128,2048]{1,0:T(8,128)(2,1)S(1)} collective-permute-done((bf16[128,2048]{1,0:T(8,128)(2,1)S(1)}, bf16[128,2048]{1,0:T(8,128)(2,1)S(1)}, u32[]{:S(2)}, u32[]{:S(2)}) %collective-permute-start) | collective-permute-done | bytes 524320 | tf_op jit(solution)/shard_map/ppermute | solution.py:74
  137.9 2.0 %collective-permute-start.1 = (bf16[128,2048]{1,0:T(8,128)(2,1)S(1)}, bf16[128,2048]{1,0:T(8,128)(2,1)S(1)}, u32[]{:S(2)}, u32[]{:S(2)}) collective-permute-start(bf16[128,2048]{1,0:T(8,128)(2,1)S(1)} %collective-permute-done), channel_id=1, source_target_pairs={{0,1},{1,2},{2,3},{3,0},{4,5},{5,6},{6,7},{7,4},{8,9},{9,10},{10,1... | collective-permute-start | bytes 1572872 | tf_op jit(solution)/shard_map/ppermute | solution.py:74
  140.0 3.5 %gather_fusion = s32[512]{0:T(512)S(1)} fusion(s32[512]{0:T(512)S(1)} %bitcast.55, s32[1024]{0:T(1024)S(1)} %get-tuple-element.11), kind=kCustom, calls=%fused_computation | custom fusion | bytes 6144 | tf_op jit(solution)/shard_map/jit(_take)/gather | solution.py:22
  143.5 1.3 gather_fusion.1
  144.8 0.6 fusion.31
  145.5 10.2 %collective-permute-done.1 = bf16[128,2048]{1,0:T(8,128)(2,1)S(1)} collective-permute-done((bf16[128,2048]{1,0:T(8,128)(2,1)S(1)}, bf16[128,2048]{1,0:T(8,128)(2,1)S(1)}, u32[]{:S(2)}, u32[]{:S(2)}) %collective-permute-start.1) | collective-permute-done | bytes 524320 | tf_op jit(solution)/shard_map/ppermute | solution.py:74
  155.7 0.6 collective-permute-start.2
  156.3 2.6 %fusion.28 = pred[128]{0:T(512)(128)(4,1)S(1)} fusion(s32[]{:T(128)} %bitcast, s32[]{:T(128)} %bitcast.1, s32[]{:T(128)} %bitcast.3, s32[]{:T(128)} %bitcast.2, s32[]{:T(128)S(6)} %mul.12), kind=kLoop, calls=%fused_computation.56 | loop fusion | flops 6272 | bytes 148 | tf_op jit(solution)/shard_map/eq | solution.py:67
  158.9 0.1 fusion.12
  159.0 15.6 %collective-permute-done.2 = bf16[128,2048]{1,0:T(8,128)(2,1)S(1)} collective-permute-done((bf16[128,2048]{1,0:T(8,128)(2,1)S(1)}, bf16[128,2048]{1,0:T(8,128)(2,1)S(1)}, u32[]{:S(2)}, u32[]{:S(2)}) %collective-permute-start.2) | collective-permute-done | bytes 524320 | tf_op jit(solution)/shard_map/ppermute | solution.py:74
  174.7 0.1 constant_dynamic-update-slice_fusion.4
  175.0 0.2 dynamic-slice_bitcast_fusion
  175.2 0.5 copy.17
  175.8 3.3 %fusion.32 = (f32[8,128]{1,0:T(8,128)S(1)}, f32[8,128,512]{2,1,0:T(8,128)}) fusion(pred[128,512]{1,0:T(8,128)(4,1)S(1)} %fusion.12, bf16[64,8,8,128]{3,2,1,0:T(8,128)(2,1)S(1)} %get-tuple-element.2, f32[128,1024]{1,0:T(8,128)} %reduce-scatter.5.cloned.1.call-done), kind=kOutput, calls=%fused_computation.61 | convolution fusion | flops 136446464 | bytes 3739648 | tf_op jit(solution)/shard_map/sub | solution.py:40
  179.1 2.2 %convolution_convert_fusion = bf16[8,128,128]{2,1,0:T(8,128)(2,1)S(1)} fusion(bf16[512,8,128]{0,2,1:T(8,128)(2,1)S(1)} %bitcast.58, f32[8,128,512]{2,1,0:T(8,128)} %get-tuple-element.9, f32[8,128]{1,0:T(8,128)S(1)} %get-tuple-element.8), kind=kOutput, calls=%fused_computation.9 | convolution fusion | flops 135397376 | bytes 3411968 | tf_op jit(solution)/shard_map/hrs,shd->rhd/dot_general | solution.py:42
  181.3 0.1 copy.16
  181.5 0.1 broadcast_select_fusion
  181.6 0.1 collective-permute-start.3
  181.6 0.1 copy.15
  181.8 0.8 broadcast_select_fusion.1
  182.6 0.6 collective-permute-done.3
  183.2 0.7 copy.52
  (26 shorter events, 0.5 us)
Async XLA Ops:
  7.2 132.8 %copy-start = (s32[1,512]{1,0:T(1,128)S(1)}, s32[1,512]{1,0:T(1,128)}, u32[]{:S(2)}) copy-start(s32[1,512]{1,0:T(1,128)} %param.6) | copy-start | bytes 6148
  7.2 44.3 %all-gather.3.cloned.1.call-start = ((), (), s32[]{:S(2)}) async-start(), calls=%async_computation.4 | async-start | bytes 2129920 | tf_op jit(solution)/shard_map/all_gather | solution.py:57
  7.9 109.5 %reduce-scatter.3.cloned.1.call-start = ((), (), s32[]{:S(2)}) async-start(), calls=%async_computation.2 | async-start | bytes 5242880 | tf_op jit(solution)/shard_map/reduce_scatter | solution.py:69
  60.6 2.7 %copy-start.2 = (f32[512,3072]{1,0:T(8,128)}, f32[512,3072]{1,0:T(8,128)S(1)}, u32[]{:S(2)}) copy-start(f32[512,3072]{1,0:T(8,128)S(1)} %fusion.2) | copy-start | bytes 18874372
  65.8 110.0 %reduce-scatter.5.cloned.1.call-start = ((), (), s32[]{:S(2)}) async-start(), calls=%async_computation.3 | async-start | bytes 2621440 | tf_op jit(solution)/shard_map/reduce_scatter | solution.py:68
  69.0 75.8 %copy-start.3 = (s32[1,4]{1,0:T(1,128)S(1)}, s32[1,4]{1,0:T(1,128)}, u32[]{:S(2)}) copy-start(s32[1,4]{1,0:T(1,128)} %param.7) | copy-start | bytes 52
  117.4 57.3 %copy-start.1 = (f32[128,2048]{1,0:T(8,128)S(1)}, f32[128,2048]{1,0:T(8,128)}, u32[]{:S(2)}) copy-start(f32[128,2048]{1,0:T(8,128)} %reduce-scatter.3.cloned.1.call-done) | copy-start | bytes 3145732
  118.8 19.2 %collective-permute-start = (bf16[128,2048]{1,0:T(8,128)(2,1)S(1)}, bf16[128,2048]{1,0:T(8,128)(2,1)S(1)}, u32[]{:S(2)}, u32[]{:S(2)}) collective-permute-start(bf16[128,2048]{1,0:T(8,128)(2,1)S(1)} %convert_element_type.29), channel_id=1, source_target_pairs={{0,1},{1,2},{2,3},{3,0},{4,5},{5,6},{6,7},{7,4},{8,9},{9,10},{10,1... | collective-permute-start | bytes 1572872 | tf_op jit(solution)/shard_map/ppermute | solution.py:74
  137.9 17.8 %collective-permute-start.1 = (bf16[128,2048]{1,0:T(8,128)(2,1)S(1)}, bf16[128,2048]{1,0:T(8,128)(2,1)S(1)}, u32[]{:S(2)}, u32[]{:S(2)}) collective-permute-start(bf16[128,2048]{1,0:T(8,128)(2,1)S(1)} %collective-permute-done), channel_id=1, source_target_pairs={{0,1},{1,2},{2,3},{3,0},{4,5},{5,6},{6,7},{7,4},{8,9},{9,10},{10,1... | collective-permute-start | bytes 1572872 | tf_op jit(solution)/shard_map/ppermute | solution.py:74
  155.7 18.9 %collective-permute-start.2 = (bf16[128,2048]{1,0:T(8,128)(2,1)S(1)}, bf16[128,2048]{1,0:T(8,128)(2,1)S(1)}, u32[]{:S(2)}, u32[]{:S(2)}) collective-permute-start(bf16[128,2048]{1,0:T(8,128)(2,1)S(1)} %collective-permute-done.1), channel_id=1, source_target_pairs={{0,1},{1,2},{2,3},{3,0},{4,5},{5,6},{6,7},{7,4},{8,9},{9,10},{10,1... | collective-permute-start | bytes 1572872 | tf_op jit(solution)/shard_map/ppermute | solution.py:74
  181.6 1.6 collective-permute-start.3
Sparse Core Ops, SparseCore 0:
  9.6 41.8 all-gather.2
  65.9 51.4 reduce-scatter.2
  120.4 49.0 reduce-scatter.4
